TPU v7x, 32 devices: a whole 2x2x4 slice. The times are simulated.
32 devices in a mesh: rows: 8 (over y, x, core), cols: 4 (over z).
Axes of the slice: x: 2, y: 2, z: 4, core: 2. Of those that a mesh axis runs over, the one named last changes fastest.
Arguments:
- irradiance_layers: bfloat16 [2, 2048, 16384], P(None, ('rows', 'cols')), may hold values from 0 to 2
- initial_heat_anomaly: float32 [2, 2048, 16384], P(None, 'rows', 'cols'), may hold values from -12 to 12
- drift_rate_eastward: float32 [2, 2048, 16384], P(None, 'rows', 'cols'), may hold values from 0.35 to 0.45
- drift_rate_northward: float32 [2, 2048, 16384], P(None, 'rows', 'cols'), may hold values from 0.33 to 0.4
- extinction_factor: float32 [2, 2048, 16384], P(None, 'rows', 'cols'), may hold values from 0.1 to 1
- windward_polarity_eastward: int32 [2, 2048], P(None, 'rows'), may hold values from 0 to 1
- windward_polarity_northward: int32 [2, 16384], P(None, 'cols'), may hold values from 0 to 1
Outputs:
- phase_slabs: float32 [2, 2048, 16384], P(None, ('rows', 'cols'))
- temperature_end: float32 [2, 2048, 16384], P(None, 'rows', 'cols')
Inputs may be any that keep to these rules, and one draw needn't show every extreme that they name: `windward_polarity_eastward`: 1 means wind plus slew toward increasing x. `windward_polarity_northward`: 1 means wind plus slew toward increasing y.
All inputs are finite; a program needn't handle non-finite values.
Results may differ from a plain program's by a relative error of at most 0.0003.
Values may be sent and summed in bfloat16 or wider, within the bound.
No kernel may reach another device: no remote copies, remote signals or barrier semaphores. Data moves between devices by JAX's collectives and lax.ppermute only.
A program may use at most 192 MiB of HBM per device.

v0:
```python
import jax
import jax.numpy as jnp
from jax import lax
from jax.sharding import PartitionSpec as P

SUBSTEPS = 4
DIFFUSION = 0.03
HEAT_RATE = 0.25


def extended(block, sides, width):
    for axis, dim in sides:
        count = lax.axis_size(axis)
        forward = [(i, i + 1) for i in range(count - 1)]
        backward = [(target, source) for source, target in forward]
        low = lax.ppermute(
            lax.slice_in_dim(block, block.shape[dim] - width, None, axis=dim), axis, forward
        )
        high = lax.ppermute(lax.slice_in_dim(block, 0, width, axis=dim), axis, backward)
        block = jnp.concatenate([low, block, high], axis=dim)
    return block


def advance(padded, wind_x, wind_y, heating):
    middle = padded[1:-1, 1:-1]
    west_cell = padded[1:-1, :-2]
    east_cell = padded[1:-1, 2:]
    south_cell = padded[:-2, 1:-1]
    north_cell = padded[2:, 1:-1]
    upwind_x = jnp.where(wind_x > 0, west_cell, east_cell)
    upwind_y = jnp.where(wind_y > 0, south_cell, north_cell)
    neighbours = west_cell + east_cell + south_cell + north_cell - 4.0 * middle
    return (
        middle
        - jnp.abs(wind_x) * (middle - upwind_x)
        - jnp.abs(wind_y) * (middle - upwind_y)
        + DIFFUSION * neighbours
        + heating
    )


def body(
    irradiance_layers,
    initial_heat_anomaly,
    drift_rate_eastward,
    drift_rate_northward,
    extinction_factor,
    windward_polarity_eastward,
    windward_polarity_northward,
):
    optical_layers = initial_heat_anomaly.shape[0]
    arrived = lax.all_to_all(irradiance_layers, "cols", split_axis=2, concat_axis=1, tiled=True)
    phases = []
    finals = []
    for optical_layer in range(optical_layers):
        light_tile = arrived[optical_layer]
        wind_x = jnp.where(
            windward_polarity_eastward[optical_layer][:, None] == 1,
            drift_rate_eastward[optical_layer],
            -drift_rate_eastward[optical_layer],
        )
        wind_y = jnp.where(
            windward_polarity_northward[optical_layer][None, :] == 1,
            drift_rate_northward[optical_layer],
            -drift_rate_northward[optical_layer],
        )
        heating = HEAT_RATE * extinction_factor[optical_layer] * light_tile.astype(jnp.float32)
        heat_transport_advance = initial_heat_anomaly[optical_layer]
        phase_sum = jnp.zeros_like(heat_transport_advance)
        for section_index in range(SUBSTEPS):
            padded = extended(heat_transport_advance, (("rows", 0), ("cols", 1)), 1)
            heat_transport_advance = advance(padded, wind_x, wind_y, heating)
            phase_sum = phase_sum + heat_transport_advance / SUBSTEPS
        phases.append(phase_sum)
        finals.append(heat_transport_advance)
    phase_slabs = lax.all_to_all(jnp.stack(phases), "cols", split_axis=1, concat_axis=2, tiled=True)
    return (phase_slabs, jnp.stack(finals))


def solution(mesh):
    return jax.shard_map(
        body,
        mesh=mesh,
        in_specs=(
            P(None, ("rows", "cols"), None),
            P(None, "rows", "cols"),
            P(None, "rows", "cols"),
            P(None, "rows", "cols"),
            P(None, "rows", "cols"),
            P(None, "rows"),
            P(None, "cols"),
        ),
        out_specs=(P(None, ("rows", "cols"), None), P(None, "rows", "cols")),
        check_vma=False,
    )
```

profile of v0, /device:TPU:3, one launch (start us, length us, event | category | flops | bytes accessed | tf_op | source)
XLA Modules:
  0.0 627.5 jit_solution(5142534280835631980)
XLA Ops:
  0.6 17.8 %copy.19 = bf16[2,64,16384]{1,0,2:T(2,128)(2,1)} copy(bf16[2,64,16384]{2,1,0:T(8,128)(2,1)} %param.7) | data formatting | bytes 8388608 | tf_op args[0]
  18.4 9.6 %reshape.44 = bf16[4,2,262144]{2,1,0:T(2,128)(2,1)} reshape(bf16[16384,2,64]{2,1,0:T(2,128)(2,1)} %bitcast.140) | data formatting | bytes 8388608
  28.0 5.0 all-to-all-start
  34.1 3.7 collective-permute-start
  37.8 1.9 collective-permute-start.1
  39.7 4.5 collective-permute-start.16
  44.3 1.9 collective-permute-start.17
  46.3 4.0 slice_bitcast_fusion.1
  50.5 3.7 collective-permute-start.2
  55.7 4.0 collective-permute-start.18
  61.0 64.7 %all-to-all-done = bf16[4,2,262144]{2,1,0:T(2,128)(2,1)} async-done(((bf16[4,2,262144]{2,1,0:T(2,128)(2,1)}), bf16[4,2,262144]{2,1,0:T(2,128)(2,1)}, u32[]{:S(2)}, u32[]{:S(2)}) %all-to-all-start) | async-done | bytes 4194336 | tf_op jit(solution)/shard_map/all_to_all | solution.py:52
  125.6 9.3 %reshape.45 = bf16[16384,2,64]{2,1,0:T(2,128)(2,1)} reshape(bf16[4,2,262144]{2,1,0:T(2,128)(2,1)} %all-to-all-done) | data formatting | bytes 8388608
  134.9 18.6 %copy.21 = bf16[2,64,4,4096]{3,1,2,0:T(8,128)(2,1)} copy(bf16[2,64,4,4096]{1,0,3,2:T(2,128)(2,1)} %bitcast.139) | data formatting | bytes 8388608 | tf_op jit(solution)/shard_map/all_to_all | solution.py:52
  153.5 4.2 fusion.15
  158.4 20.0 %add_add_fusion.7 = (f32[256,4096]{1,0:T(8,128)S(1)}, pred[256,4096]{1,0:T(8,128)(4,1)}, pred[256,4096]{1,0:T(8,128)(4,1)}) fusion(f32[256,4096]{1,0:T(8,128)} %copy-done.8, f32[1,4096]{1,0:T(1,128)S(1)} %collective-permute-done, f32[1,4096]{1,0:T(1,128)S(1)} %collective-permute-done.1, f32[258,1]{1,0:T(8,128)} %copy-done.12, f32[258,1]{1,0:T(8,128)} %copy-done.13, ...), kind=kLoop, calls=%fused_computation.82 | loop fusion | flops 36700160 | bytes 25205008 | tf_op jit(solution)/shard_map/add | solution.py:34
  178.5 5.6 collective-permute-start.4
  184.1 1.9 collective-permute-start.5
  186.2 19.6 %add_add_fusion.3 = (f32[256,4096]{1,0:T(8,128)S(1)}, pred[256,4096]{1,0:T(8,128)(4,1)}, pred[256,4096]{1,0:T(8,128)(4,1)}) fusion(f32[256,4096]{1,0:T(8,128)} %copy-done.7, f32[1,4096]{1,0:T(1,128)S(1)} %collective-permute-done.16, f32[1,4096]{1,0:T(1,128)S(1)} %collective-permute-done.17, f32[258,1]{1,0:T(8,128)S(1)} %collective-permute-done.18, ...), kind=kLoop, calls=%fused_computation.76 | loop fusion | flops 36700160 | bytes 25205008 | tf_op jit(solution)/shard_map/add | solution.py:34
  205.8 4.5 collective-permute-start.20
  210.3 1.9 collective-permute-start.21
  216.4 2.9 collective-permute-start.22
  221.9 12.6 %add_add_fusion.6 = f32[256,4096]{1,0:T(8,128)} fusion(f32[256,4096]{1,0:T(8,128)S(1)} %get-tuple-element.8, pred[256,4096]{1,0:T(8,128)(4,1)} %get-tuple-element.10, f32[1,4096]{1,0:T(1,128)S(1)} %collective-permute-done.4, f32[1,4096]{1,0:T(1,128)S(1)} %collective-permute-done.5, pred[256,4096]{1,0:T(8,128)(4,1)} %get-tuple-element.9, ...), kind=kLoop, calls=%fused_computation.81 | loop fusion | flops 34603008 | bytes 25205008 | tf_op jit(solution)/shard_map/add | solution.py:34
  236.2 5.1 collective-permute-start.8
  241.3 1.9 collective-permute-start.9
  243.2 18.1 %add_add_fusion.2 = f32[256,4096]{1,0:T(8,128)} fusion(f32[256,4096]{1,0:T(8,128)} %copy-done, pred[256,4096]{1,0:T(8,128)(4,1)} %get-tuple-element.15, f32[1,4096]{1,0:T(1,128)S(1)} %collective-permute-done.20, f32[1,4096]{1,0:T(1,128)} %copy-done.22, pred[256,4096]{1,0:T(8,128)(4,1)} %get-tuple-element.14, f32[258,1]{1,0:T(8,128)S(1)} %collective-permute-done.22, ...), kind=kLoop, calls=%fused_computation.75 | loop fusion | flops 34603008 | bytes 25205008 | tf_op jit(solution)/shard_map/add | solution.py:34
  262.4 4.7 collective-permute-start.24
  267.1 1.9 collective-permute-start.25
  270.1 4.3 collective-permute-start.10
  276.3 4.0 collective-permute-start.26
  282.5 18.8 %add_add_fusion.5 = f32[256,4096]{1,0:T(8,128)} fusion(f32[256,4096]{1,0:T(8,128)} %add_add_fusion.6, pred[256,4096]{1,0:T(8,128)(4,1)} %get-tuple-element.10, f32[1,4096]{1,0:T(1,128)S(1)} %collective-permute-done.8, f32[1,4096]{1,0:T(1,128)S(1)} %collective-permute-done.9, pred[256,4096]{1,0:T(8,128)(4,1)} %get-tuple-element.9, f32[258,1]{1,0:T(8,128)} %copy-done.15, ...), kind=kLoop, calls=%fused_computation.80 | loop fusion | flops 34603008 | bytes 25205008 | tf_op jit(solution)/shard_map/add | solution.py:34
  302.9 5.4 collective-permute-start.12
  308.3 1.9 collective-permute-start.13
  310.2 18.1 %add_add_fusion.1 = f32[256,4096]{1,0:T(8,128)} fusion(f32[256,4096]{1,0:T(8,128)} %add_add_fusion.2, pred[256,4096]{1,0:T(8,128)(4,1)} %get-tuple-element.15, f32[1,4096]{1,0:T(1,128)S(1)} %collective-permute-done.24, f32[1,4096]{1,0:T(1,128)} %copy-done.23, pred[256,4096]{1,0:T(8,128)(4,1)} %get-tuple-element.14, f32[258,1]{1,0:T(8,128)S(1)} %collective-permute-done.26, ...), kind=kLoop, calls=%fused_computation.74 | loop fusion | flops 34603008 | bytes 25205008 | tf_op jit(solution)/shard_map/add | solution.py:34
  329.3 4.5 collective-permute-start.28
  333.9 2.3 collective-permute-start.29
  337.4 4.3 collective-permute-start.14
  343.1 1.8 pad_maximum_fusion.68
  344.8 4.8 collective-permute-start.30
  351.4 20.9 %multiply_bitcast_fusion = (f32[1,256,4096]{2,1,0:T(8,128)}, f32[256,4096]{1,0:T(8,128)}) fusion(f32[256,4096]{1,0:T(8,128)} %add_add_fusion.5, f32[256,4096]{1,0:T(8,128)S(1)} %get-tuple-element.8, f32[256,4096]{1,0:T(8,128)S(1)} %copy-done.2, bf16[1,4,64,4096]{3,2,1,0:T(8,128)(2,1)S(1)} %copy-done.6, f32[2,256,4096]{2,1,0:T(8,128)} %param.11, ...), kind=kLoop, calls=%fused_computation.78 | loop fusion | flops 38797312 | bytes 37787920 | tf_op jit(solution)/shard_map/stack | solution.py:76
  372.3 8.7 %copy.22 = f32[1,256,4096]{2,0,1:T(1,128)} copy(f32[1,256,4096]{2,1,0:T(8,128)} %get-tuple-element.6) | data formatting | bytes 8388608 | tf_op jit(solution)/shard_map/stack | solution.py:76
  381.1 19.5 %add_multiply_fusion = (f32[256,4096]{1,0:T(8,128)S(1)}, f32[256,4096]{1,0:T(8,128)}) fusion(f32[256,4096]{1,0:T(8,128)} %add_add_fusion.1, f32[256,4096]{1,0:T(8,128)S(1)} %copy-done.1, f32[256,4096]{1,0:T(8,128)} %add_add_fusion.2, bf16[1,4,64,4096]{3,2,1,0:T(8,128)(2,1)S(1)} %copy-done.4, f32[2,256,4096]{2,1,0:T(8,128)} %param.11, ...), kind=kLoop, calls=%fused_computation.72 | loop fusion | flops 38797312 | bytes 37787920 | tf_op jit(solution)/shard_map/add | solution.py:73
  400.6 4.6 stack.19
  405.2 9.2 %pad_maximum_fusion = f32[2,256,4096]{2,0,1:T(2,128)} fusion(f32[1,256,4096]{2,0,1:T(1,128)S(1)} %stack.19, f32[1,256,4096]{2,0,1:T(1,128)S(1)} %copy-done.11), kind=kLoop, calls=%fused_computation | loop fusion | flops 2097152 | bytes 16777216 | tf_op jit(solution)/shard_map/stack | solution.py:76
  414.4 6.8 %all-to-all-start.1 = ((f32[2,256,4096]{2,0,1:T(2,128)}), f32[2,256,4096]{2,0,1:T(2,128)}, u32[]{:S(2)}, u32[]{:S(2)}) async-start(f32[2,256,4096]{2,0,1:T(2,128)} %pad_maximum_fusion), calls=%async_computation.1 | async-start | bytes 16777216 | tf_op jit(solution)/shard_map/all_to_all | solution.py:76
  421.2 7.9 %pad_maximum_fusion.1 = f32[2,256,4096]{2,1,0:T(8,128)} fusion(f32[1,256,4096]{2,1,0:T(8,128)} %bitcast.143, f32[1,256,4096]{2,1,0:T(8,128)} %bitcast.142), kind=kLoop, calls=%fused_computation.1 | loop fusion | flops 2097152 | bytes 16777216 | tf_op jit(solution)/shard_map/stack | solution.py:77
  429.0 175.3 %all-to-all-done.1 = f32[2,256,4096]{2,0,1:T(2,128)} async-done(((f32[2,256,4096]{2,0,1:T(2,128)}), f32[2,256,4096]{2,0,1:T(2,128)}, u32[]{:S(2)}, u32[]{:S(2)}) %all-to-all-start.1) | async-done | bytes 8388640 | tf_op jit(solution)/shard_map/all_to_all | solution.py:76
  604.3 12.1 %copy.23 = f32[2,64,4,4096]{3,2,1,0:T(4,128)} copy(f32[2,64,4,4096]{3,0,1,2:T(2,128)} %bitcast.18) | data formatting | bytes 16777216 | tf_op jit(solution)/shard_map/all_to_all | solution.py:76
  616.4 10.9 %all_to_all.30 = f32[2,64,16384]{2,1,0:T(8,128)} reshape(f32[2,64,4,4096]{3,2,1,0:T(4,128)} %copy.23) | data formatting | bytes 16777216 | tf_op jit(solution)/shard_map/all_to_all | solution.py:76
  (128 shorter events, 26.2 us)
Async XLA Ops:
  28.0 18.2 %copy-start.24 = (s32[2,4096]{1,0:T(2,128)S(1)}, s32[2,4096]{1,0:T(2,128)}, u32[]{:S(2)}) copy-start(s32[2,4096]{1,0:T(2,128)} %param.13) | copy-start | bytes 98308
  28.0 97.7 %all-to-all-start = ((bf16[4,2,262144]{2,1,0:T(2,128)(2,1)}), bf16[4,2,262144]{2,1,0:T(2,128)(2,1)}, u32[]{:S(2)}, u32[]{:S(2)}) async-start(bf16[4,2,262144]{2,1,0:T(2,128)(2,1)} %reshape.44), calls=%async_computation | async-start | bytes 8388608 | tf_op jit(solution)/shard_map/all_to_all | solution.py:52
  34.1 16.3 %collective-permute-start = (f32[1,4096]{1,0:T(1,128)S(1)}, f32[1,4096]{1,0:T(1,128)S(1)}, u32[]{:S(2)}, u32[]{:S(2)}) collective-permute-start(f32[1,4096]{1,0:T(1,128)S(1)} %get-tuple-element.17), channel_id=1, source_target_pairs={{0,4},{4,8},{8,12},{12,16},{16,20},{20,24},{24,28},{1,5},{5,9},{9,... | collective-permute-start | bytes 49160 | tf_op jit(solution)/shard_map/ppermute | solution.py:16
  37.8 12.6 %collective-permute-start.1 = (f32[1,4096]{1,0:T(1,128)S(1)}, f32[1,4096]{1,0:T(1,128)S(1)}, u32[]{:S(2)}, u32[]{:S(2)}) collective-permute-start(f32[1,4096]{1,0:T(1,128)S(1)} %get-tuple-element.16), channel_id=1, source_target_pairs={{4,0},{8,4},{12,8},{16,12},{20,16},{24,20},{28,24},{5,1},{9,5},{13... | collective-permute-start | bytes 49160 | tf_op jit(solution)/shard_map/ppermute | solution.py:19
  39.7 15.8 %collective-permute-start.16 = (f32[1,4096]{1,0:T(1,128)S(1)}, f32[1,4096]{1,0:T(1,128)S(1)}, u32[]{:S(2)}, u32[]{:S(2)}) collective-permute-start(f32[1,4096]{1,0:T(1,128)S(1)} %get-tuple-element.19), channel_id=1, source_target_pairs={{0,4},{4,8},{8,12},{12,16},{16,20},{20,24},{24,28},{1,5},{5,9},{9,... | collective-permute-start | bytes 49160 | tf_op jit(solution)/shard_map/ppermute | solution.py:16
  44.3 11.3 %collective-permute-start.17 = (f32[1,4096]{1,0:T(1,128)S(1)}, f32[1,4096]{1,0:T(1,128)S(1)}, u32[]{:S(2)}, u32[]{:S(2)}) collective-permute-start(f32[1,4096]{1,0:T(1,128)S(1)} %get-tuple-element.18), channel_id=1, source_target_pairs={{4,0},{8,4},{12,8},{16,12},{20,16},{24,20},{28,24},{5,1},{9,5},{13... | collective-permute-start | bytes 49160 | tf_op jit(solution)/shard_map/ppermute | solution.py:19
  50.4 232.1 %copy-start.25 = (pred[256]{0:T(512)(128)(4,1)}, pred[256]{0:T(512)(128)(4,1)S(1)}, u32[]{:S(2)}) copy-start(pred[256]{0:T(512)(128)(4,1)S(1)} %get-tuple-element.4) | copy-start | bytes 772
  50.5 107.2 %collective-permute-start.2 = (f32[258,1]{1,0:T(8,128)S(1)}, f32[258,1]{1,0:T(8,128)S(1)}, u32[]{:S(2)}, u32[]{:S(2)}) collective-permute-start(f32[258,1]{1,0:T(8,128)S(1)} %get-tuple-element.29), channel_id=1, source_target_pairs={{0,1},{1,2},{2,3},{4,5},{5,6},{6,7},{8,9},{9,10},{10,11},{12,13},{... | collective-permute-start | bytes 3104 | tf_op jit(solution)/shard_map/ppermute | solution.py:16
  54.2 103.5 %collective-permute-start.3 = (f32[258,1]{1,0:T(8,128)S(1)}, f32[258,1]{1,0:T(8,128)S(1)}, u32[]{:S(2)}, u32[]{:S(2)}) collective-permute-start(f32[258,1]{1,0:T(8,128)S(1)} %get-tuple-element.28), channel_id=1, source_target_pairs={{1,0},{2,1},{3,2},{5,4},{6,5},{7,6},{9,8},{10,9},{11,10},{13,12},{... | collective-permute-start | bytes 3104 | tf_op jit(solution)/shard_map/ppermute | solution.py:19
  55.7 130.4 %collective-permute-start.18 = (f32[258,1]{1,0:T(8,128)S(1)}, f32[258,1]{1,0:T(8,128)S(1)}, u32[]{:S(2)}, u32[]{:S(2)}) collective-permute-start(f32[258,1]{1,0:T(8,128)S(1)} %get-tuple-element.37), channel_id=1, source_target_pairs={{0,1},{1,2},{2,3},{4,5},{5,6},{6,7},{8,9},{9,10},{10,11},{12,13},{... | collective-permute-start | bytes 3104 | tf_op jit(solution)/shard_map/ppermute | solution.py:16
  59.7 126.4 %collective-permute-start.19 = (f32[258,1]{1,0:T(8,128)S(1)}, f32[258,1]{1,0:T(8,128)}, u32[]{:S(2)}, u32[]{:S(2)}) collective-permute-start(f32[258,1]{1,0:T(8,128)S(1)} %get-tuple-element.36), channel_id=1, source_target_pairs={{1,0},{2,1},{3,2},{5,4},{6,5},{7,6},{9,8},{10,9},{11,10},{13,12},{... | collective-permute-start | bytes 3104 | tf_op jit(solution)/shard_map/ppermute | solution.py:19
  153.5 32.6 %slice-start = ((s8[8388608]{0:T(1024)(128)(4,1)}), s8[4194304]{0:T(1024)(128)(4,1)S(1)}, s32[]{:S(2)}) async-start(s8[8388608]{0:T(1024)(128)(4,1)} %bitcast.133), calls=%async_computation.2 | async-start | bytes 8388608
  153.5 32.6 %slice-start.2 = ((s8[8388608]{0:T(1024)(128)(4,1)}), s8[4194304]{0:T(1024)(128)(4,1)S(1)}, s32[]{:S(2)}) async-start(s8[8388608]{0:T(1024)(128)(4,1)} %bitcast.135), calls=%async_computation.4 | async-start | bytes 8388608
  153.5 32.6 %slice-start.4 = ((s8[8388608]{0:T(1024)(128)(4,1)}), s8[4194304]{0:T(1024)(128)(4,1)S(1)}, s32[]{:S(2)}) async-start(s8[8388608]{0:T(1024)(128)(4,1)} %bitcast.137), calls=%async_computation.6 | async-start | bytes 8388608
  157.7 20.8 %copy-start.5 = (bf16[1,4,64,4096]{3,2,1,0:T(8,128)(2,1)}, bf16[1,4,64,4096]{3,2,1,0:T(8,128)(2,1)S(1)}, u32[]{:S(2)}) copy-start(bf16[1,4,64,4096]{3,2,1,0:T(8,128)(2,1)S(1)} %get-tuple-element.44) | copy-start | bytes 6291460
  158.4 27.7 %slice-start.1 = ((s8[8388608]{0:T(1024)(128)(4,1)}), s8[4194304]{0:T(1024)(128)(4,1)S(1)}, s32[]{:S(2)}) async-start(s8[8388608]{0:T(1024)(128)(4,1)} %bitcast.133), calls=%async_computation.3 | async-start | bytes 8388608
  158.4 27.7 %slice-start.3 = ((s8[8388608]{0:T(1024)(128)(4,1)}), s8[4194304]{0:T(1024)(128)(4,1)S(1)}, s32[]{:S(2)}) async-start(s8[8388608]{0:T(1024)(128)(4,1)} %bitcast.135), calls=%async_computation.5 | async-start | bytes 8388608
  158.4 27.7 %slice-start.5 = ((s8[8388608]{0:T(1024)(128)(4,1)}), s8[4194304]{0:T(1024)(128)(4,1)S(1)}, s32[]{:S(2)}) async-start(s8[8388608]{0:T(1024)(128)(4,1)} %bitcast.137), calls=%async_computation.7 | async-start | bytes 8388608
  178.5 33.7 %collective-permute-start.4 = (f32[1,4096]{1,0:T(1,128)S(1)}, f32[1,4096]{1,0:T(1,128)S(1)}, u32[]{:S(2)}, u32[]{:S(2)}) collective-permute-start(f32[1,4096]{1,0:T(1,128)S(1)} %get-tuple-element.43), channel_id=1, source_target_pairs={{0,4},{4,8},{8,12},{12,16},{16,20},{20,24},{24,28},{1,5},{5,9},{9,... | collective-permute-start | bytes 49160 | tf_op jit(solution)/shard_map/ppermute | solution.py:16
  184.1 28.1 %collective-permute-start.5 = (f32[1,4096]{1,0:T(1,128)S(1)}, f32[1,4096]{1,0:T(1,128)S(1)}, u32[]{:S(2)}, u32[]{:S(2)}) collective-permute-start(f32[1,4096]{1,0:T(1,128)S(1)} %get-tuple-element.42), channel_id=1, source_target_pairs={{4,0},{8,4},{12,8},{16,12},{20,16},{24,20},{28,24},{5,1},{9,5},{13... | collective-permute-start | bytes 49160 | tf_op jit(solution)/shard_map/ppermute | solution.py:19
  205.8 9.2 %collective-permute-start.20 = (f32[1,4096]{1,0:T(1,128)S(1)}, f32[1,4096]{1,0:T(1,128)S(1)}, u32[]{:S(2)}, u32[]{:S(2)}) collective-permute-start(f32[1,4096]{1,0:T(1,128)S(1)} %get-tuple-element.51), channel_id=1, source_target_pairs={{0,4},{4,8},{8,12},{12,16},{16,20},{20,24},{24,28},{1,5},{5,9},{9,... | collective-permute-start | bytes 49160 | tf_op jit(solution)/shard_map/ppermute | solution.py:16
  210.3 6.0 collective-permute-start.21
  212.4 8.2 %collective-permute-start.6 = (f32[258,1]{1,0:T(8,128)S(1)}, f32[258,1]{1,0:T(8,128)S(1)}, u32[]{:S(2)}, u32[]{:S(2)}) collective-permute-start(f32[258,1]{1,0:T(8,128)S(1)} %get-tuple-element.27), channel_id=1, source_target_pairs={{0,1},{1,2},{2,3},{4,5},{5,6},{6,7},{8,9},{9,10},{10,11},{12,13},{... | collective-permute-start | bytes 3104 | tf_op jit(solution)/shard_map/ppermute | solution.py:16
  213.7 7.3 %collective-permute-start.7 = (f32[258,1]{1,0:T(8,128)S(1)}, f32[258,1]{1,0:T(8,128)S(1)}, u32[]{:S(2)}, u32[]{:S(2)}) collective-permute-start(f32[258,1]{1,0:T(8,128)S(1)} %get-tuple-element.26), channel_id=1, source_target_pairs={{1,0},{2,1},{3,2},{5,4},{6,5},{7,6},{9,8},{10,9},{11,10},{13,12},{... | collective-permute-start | bytes 3104 | tf_op jit(solution)/shard_map/ppermute | solution.py:19
  216.3 18.3 %copy-start.22 = (f32[1,4096]{1,0:T(1,128)}, f32[1,4096]{1,0:T(1,128)S(1)}, u32[]{:S(2)}) copy-start(f32[1,4096]{1,0:T(1,128)S(1)} %collective-permute-done.21) | copy-start | bytes 49156
  216.4 26.8 %collective-permute-start.22 = (f32[258,1]{1,0:T(8,128)S(1)}, f32[258,1]{1,0:T(8,128)S(1)}, u32[]{:S(2)}, u32[]{:S(2)}) collective-permute-start(f32[258,1]{1,0:T(8,128)S(1)} %get-tuple-element.35), channel_id=1, source_target_pairs={{0,1},{1,2},{2,3},{4,5},{5,6},{6,7},{8,9},{9,10},{10,11},{12,13},{... | collective-permute-start | bytes 3104 | tf_op jit(solution)/shard_map/ppermute | solution.py:16
  219.3 23.9 %collective-permute-start.23 = (f32[258,1]{1,0:T(8,128)S(1)}, f32[258,1]{1,0:T(8,128)}, u32[]{:S(2)}, u32[]{:S(2)}) collective-permute-start(f32[258,1]{1,0:T(8,128)S(1)} %get-tuple-element.34), channel_id=1, source_target_pairs={{1,0},{2,1},{3,2},{5,4},{6,5},{7,6},{9,8},{10,9},{11,10},{13,12},{... | collective-permute-start | bytes 3104 | tf_op jit(solution)/shard_map/ppermute | solution.py:19
  236.2 32.9 %collective-permute-start.8 = (f32[1,4096]{1,0:T(1,128)}, f32[1,4096]{1,0:T(1,128)S(1)}, u32[]{:S(2)}, u32[]{:S(2)}) collective-permute-start(f32[1,4096]{1,0:T(1,128)} %get-tuple-element.41), channel_id=1, source_target_pairs={{0,4},{4,8},{8,12},{12,16},{16,20},{20,24},{24,28},{1,5},{5,9},{9,... | collective-permute-start | bytes 49160 | tf_op jit(solution)/shard_map/ppermute | solution.py:16
  241.3 27.8 %collective-permute-start.9 = (f32[1,4096]{1,0:T(1,128)}, f32[1,4096]{1,0:T(1,128)S(1)}, u32[]{:S(2)}, u32[]{:S(2)}) collective-permute-start(f32[1,4096]{1,0:T(1,128)} %get-tuple-element.40), channel_id=1, source_target_pairs={{4,0},{8,4},{12,8},{16,12},{20,16},{24,20},{28,24},{5,1},{9,5},{13... | collective-permute-start | bytes 49160 | tf_op jit(solution)/shard_map/ppermute | solution.py:19
  262.4 13.3 %collective-permute-start.24 = (f32[1,4096]{1,0:T(1,128)S(1)}, f32[1,4096]{1,0:T(1,128)S(1)}, u32[]{:S(2)}, u32[]{:S(2)}) collective-permute-start(f32[1,4096]{1,0:T(1,128)S(1)} %get-tuple-element.49), channel_id=1, source_target_pairs={{0,4},{4,8},{8,12},{12,16},{16,20},{20,24},{24,28},{1,5},{5,9},{9,... | collective-permute-start | bytes 49160 | tf_op jit(solution)/shard_map/ppermute | solution.py:16
  267.1 8.6 %collective-permute-start.25 = (f32[1,4096]{1,0:T(1,128)S(1)}, f32[1,4096]{1,0:T(1,128)S(1)}, u32[]{:S(2)}, u32[]{:S(2)}) collective-permute-start(f32[1,4096]{1,0:T(1,128)S(1)} %get-tuple-element.48), channel_id=1, source_target_pairs={{4,0},{8,4},{12,8},{16,12},{20,16},{24,20},{28,24},{5,1},{9,5},{13... | collective-permute-start | bytes 49160 | tf_op jit(solution)/shard_map/ppermute | solution.py:19
  270.1 11.7 %collective-permute-start.10 = (f32[258,1]{1,0:T(8,128)S(1)}, f32[258,1]{1,0:T(8,128)S(1)}, u32[]{:S(2)}, u32[]{:S(2)}) collective-permute-start(f32[258,1]{1,0:T(8,128)S(1)} %get-tuple-element.25), channel_id=1, source_target_pairs={{0,1},{1,2},{2,3},{4,5},{5,6},{6,7},{8,9},{9,10},{10,11},{12,13},{... | collective-permute-start | bytes 3104 | tf_op jit(solution)/shard_map/ppermute | solution.py:16
  274.4 8.1 %collective-permute-start.11 = (f32[258,1]{1,0:T(8,128)S(1)}, f32[258,1]{1,0:T(8,128)}, u32[]{:S(2)}, u32[]{:S(2)}) collective-permute-start(f32[258,1]{1,0:T(8,128)S(1)} %get-tuple-element.24), channel_id=1, source_target_pairs={{1,0},{2,1},{3,2},{5,4},{6,5},{7,6},{9,8},{10,9},{11,10},{13,12},{... | collective-permute-start | bytes 3104 | tf_op jit(solution)/shard_map/ppermute | solution.py:19
  276.3 33.9 %collective-permute-start.26 = (f32[258,1]{1,0:T(8,128)S(1)}, f32[258,1]{1,0:T(8,128)S(1)}, u32[]{:S(2)}, u32[]{:S(2)}) collective-permute-start(f32[258,1]{1,0:T(8,128)S(1)} %get-tuple-element.33), channel_id=1, source_target_pairs={{0,1},{1,2},{2,3},{4,5},{5,6},{6,7},{8,9},{9,10},{10,11},{12,13},{... | collective-permute-start | bytes 3104 | tf_op jit(solution)/shard_map/ppermute | solution.py:16
  280.3 29.9 %collective-permute-start.27 = (f32[258,1]{1,0:T(8,128)S(1)}, f32[258,1]{1,0:T(8,128)}, u32[]{:S(2)}, u32[]{:S(2)}) collective-permute-start(f32[258,1]{1,0:T(8,128)S(1)} %get-tuple-element.32), channel_id=1, source_target_pairs={{1,0},{2,1},{3,2},{5,4},{6,5},{7,6},{9,8},{10,9},{11,10},{13,12},{... | collective-permute-start | bytes 3104 | tf_op jit(solution)/shard_map/ppermute | solution.py:19
  302.9 33.3 %collective-permute-start.12 = (f32[1,4096]{1,0:T(1,128)}, f32[1,4096]{1,0:T(1,128)S(1)}, u32[]{:S(2)}, u32[]{:S(2)}) collective-permute-start(f32[1,4096]{1,0:T(1,128)} %get-tuple-element.38), channel_id=1, source_target_pairs={{0,4},{4,8},{8,12},{12,16},{16,20},{20,24},{24,28},{1,5},{5,9},{9,... | collective-permute-start | bytes 49160 | tf_op jit(solution)/shard_map/ppermute | solution.py:16
  308.3 28.0 %collective-permute-start.13 = (f32[1,4096]{1,0:T(1,128)S(1)}, f32[1,4096]{1,0:T(1,128)S(1)}, u32[]{:S(2)}, u32[]{:S(2)}) collective-permute-start(f32[1,4096]{1,0:T(1,128)S(1)} %get-tuple-element.39), channel_id=1, source_target_pairs={{4,0},{8,4},{12,8},{16,12},{20,16},{24,20},{28,24},{5,1},{9,5},{13... | collective-permute-start | bytes 49160 | tf_op jit(solution)/shard_map/ppermute | solution.py:19
  329.3 13.7 %collective-permute-start.28 = (f32[1,4096]{1,0:T(1,128)S(1)}, f32[1,4096]{1,0:T(1,128)S(1)}, u32[]{:S(2)}, u32[]{:S(2)}) collective-permute-start(f32[1,4096]{1,0:T(1,128)S(1)} %get-tuple-element.46), channel_id=1, source_target_pairs={{0,4},{4,8},{8,12},{12,16},{16,20},{20,24},{24,28},{1,5},{5,9},{9,... | collective-permute-start | bytes 49160 | tf_op jit(solution)/shard_map/ppermute | solution.py:16
  333.9 17.4 %copy-start.2 = (f32[256,4096]{1,0:T(8,128)S(1)}, f32[256,4096]{1,0:T(8,128)}, u32[]{:S(2)}) copy-start(f32[256,4096]{1,0:T(8,128)} %add_add_fusion.6) | copy-start | bytes 12582916
  333.9 17.4 %copy-start.6 = (bf16[1,4,64,4096]{3,2,1,0:T(8,128)(2,1)S(1)}, bf16[1,4,64,4096]{3,2,1,0:T(8,128)(2,1)}, u32[]{:S(2)}) copy-start(bf16[1,4,64,4096]{3,2,1,0:T(8,128)(2,1)} %copy-done.5) | copy-start | bytes 6291460
  333.9 9.1 %collective-permute-start.29 = (f32[1,4096]{1,0:T(1,128)S(1)}, f32[1,4096]{1,0:T(1,128)S(1)}, u32[]{:S(2)}, u32[]{:S(2)}) collective-permute-start(f32[1,4096]{1,0:T(1,128)S(1)} %get-tuple-element.47), channel_id=1, source_target_pairs={{4,0},{8,4},{12,8},{16,12},{20,16},{24,20},{28,24},{5,1},{9,5},{13... | collective-permute-start | bytes 49160 | tf_op jit(solution)/shard_map/ppermute | solution.py:19
  337.4 13.9 %collective-permute-start.14 = (f32[258,1]{1,0:T(8,128)S(1)}, f32[258,1]{1,0:T(8,128)S(1)}, u32[]{:S(2)}, u32[]{:S(2)}) collective-permute-start(f32[258,1]{1,0:T(8,128)S(1)} %get-tuple-element.22), channel_id=1, source_target_pairs={{0,1},{1,2},{2,3},{4,5},{5,6},{6,7},{8,9},{9,10},{10,11},{12,13},{... | collective-permute-start | bytes 3104 | tf_op jit(solution)/shard_map/ppermute | solution.py:16
  341.7 9.6 %collective-permute-start.15 = (f32[258,1]{1,0:T(8,128)S(1)}, f32[258,1]{1,0:T(8,128)S(1)}, u32[]{:S(2)}, u32[]{:S(2)}) collective-permute-start(f32[258,1]{1,0:T(8,128)S(1)} %get-tuple-element.23), channel_id=1, source_target_pairs={{1,0},{2,1},{3,2},{5,4},{6,5},{7,6},{9,8},{10,9},{11,10},{13,12},{... | collective-permute-start | bytes 3104 | tf_op jit(solution)/shard_map/ppermute | solution.py:19
  343.0 29.3 %copy-start.17 = (f32[1,4096]{1,0:T(1,128)}, f32[1,4096]{1,0:T(1,128)S(1)}, u32[]{:S(2)}) copy-start(f32[1,4096]{1,0:T(1,128)S(1)} %collective-permute-done.28) | copy-start | bytes 49156
  343.1 29.2 %copy-start.21 = (f32[1,4096]{1,0:T(1,128)}, f32[1,4096]{1,0:T(1,128)S(1)}, u32[]{:S(2)}) copy-start(f32[1,4096]{1,0:T(1,128)S(1)} %collective-permute-done.29) | copy-start | bytes 49156
  344.8 36.2 %collective-permute-start.30 = (f32[258,1]{1,0:T(8,128)}, f32[258,1]{1,0:T(8,128)S(1)}, u32[]{:S(2)}, u32[]{:S(2)}) collective-permute-start(f32[258,1]{1,0:T(8,128)} %get-tuple-element.30), channel_id=1, source_target_pairs={{0,1},{1,2},{2,3},{4,5},{5,6},{6,7},{8,9},{9,10},{10,11},{12,13},{... | collective-permute-start | bytes 3104 | tf_op jit(solution)/shard_map/ppermute | solution.py:16
  349.6 31.4 %collective-permute-start.31 = (f32[258,1]{1,0:T(8,128)S(1)}, f32[258,1]{1,0:T(8,128)S(1)}, u32[]{:S(2)}, u32[]{:S(2)}) collective-permute-start(f32[258,1]{1,0:T(8,128)S(1)} %get-tuple-element.31), channel_id=1, source_target_pairs={{1,0},{2,1},{3,2},{5,4},{6,5},{7,6},{9,8},{10,9},{11,10},{13,12},{... | collective-permute-start | bytes 3104 | tf_op jit(solution)/shard_map/ppermute | solution.py:19
  414.4 189.9 %all-to-all-start.1 = ((f32[2,256,4096]{2,0,1:T(2,128)}), f32[2,256,4096]{2,0,1:T(2,128)}, u32[]{:S(2)}, u32[]{:S(2)}) async-start(f32[2,256,4096]{2,0,1:T(2,128)} %pad_maximum_fusion), calls=%async_computation.1 | async-start | bytes 16777216 | tf_op jit(solution)/shard_map/all_to_all | solution.py:76
  (20 other events, 141.7 us)
where the time goes:
time: 638 us; the launch traced here: 628 us
  waiting for transfers between devices  242 us (38%)
  other arithmetic  169 us (26%)
  local copies, waits for them, and re-layouts  109 us (17%)
  starting transfers between devices  106 us (17%)
    all_to_all x1, waiting for transfers between devices, body(): lax.all_to_all(jnp.stack(phases), 'cols', split_axis=1, concat_axis=2, ti...  175 us
    add x6, other arithmetic, advance(): middle - jnp.abs(wind_x) * (middle - upwind_x)  107 us
    ppermute x16, starting transfers between devices, extended(): lax.ppermute(lax.slice_in_dim(block, block.shape[dim] - width, None, axis...  67.2 us
    all_to_all x1, waiting for transfers between devices, body(): lax.all_to_all(irradiance_layers, 'cols', split_axis=2, concat_axis=1, ti...  64.7 us
    unnamed x71, local copies, waits for them, and re-layouts  39.5 us
    another operation x2, other arithmetic, body(): jnp.stack(phases)  30.1 us
    ppermute x16, starting transfers between devices, extended(): lax.ppermute(lax.slice_in_dim(block, 0, width, axis=dim), axis, backward)  26.7 us
    all_to_all x2, local copies, waits for them, and re-layouts, body(): lax.all_to_all(jnp.stack(phases), 'cols', split_axis=1, concat_axis=2, ti...  23 us
  transfers between devices with their start and end apart: 34, of which 4 were waited for; matrix products, arithmetic and copies ran while one was open for 31% of the time, Pallas kernels for 0%

commit v1 on v0

--- a/solution.py
+++ b/solution.py
@@ -73,7 +73,12 @@
             phase_sum = phase_sum + heat_transport_advance / SUBSTEPS
         phases.append(phase_sum)
         finals.append(heat_transport_advance)
-    phase_slabs = lax.all_to_all(jnp.stack(phases), "cols", split_axis=1, concat_axis=2, tiled=True)
+    phase_slabs = jnp.concatenate(
+        lax.all_to_all(
+            jnp.stack(jnp.split(jnp.stack(phases), lax.axis_size("cols"), axis=1)), "cols", 0, 0
+        ),
+        axis=2,
+    )
     return (phase_slabs, jnp.stack(finals))
 
 

time: 638 us -> 607 us (0.951)
  local copies, waits for them, and re-layouts: 109 us -> 80.5 us
    all_to_all x2 -> x0, local copies, waits for them, and re-layouts: 23 us -> none  [body(): lax.all_to_all(jnp.stack(phases), 'cols', split_axis=1, concat_axis=2, ti...]
    add x1 -> x0, other arithmetic: 19.5 us -> none  [body(): phase_sum = phase_sum + heat_transport_advance / SUBSTEPS]
    another operation x2 -> x0, local copies, waits for them, and re-layouts: 13.3 us -> none  [body(): jnp.stack(phases)]
    another operation x2, other arithmetic: 30.1 us -> 41.6 us  [body(): jnp.stack(phases)]
    reshape x0 -> x1, local copies, waits for them, and re-layouts: none -> 7.77 us  [body(): jnp.concatenate(lax.all_to_all(jnp.stack(jnp.split(jnp.stack(phases), lax...]
    unnamed x71 -> x57, local copies, waits for them, and re-layouts: 39.5 us -> 39.3 us
where the time goes in v1:
time: 607 us; the launch traced here: 596 us
  waiting for transfers between devices  242 us (40%)
  other arithmetic  167 us (28%)
  starting transfers between devices  105 us (17%)
  local copies, waits for them, and re-layouts  80.5 us (13%)
    all_to_all x1, waiting for transfers between devices, body(): lax.all_to_all(jnp.stack(jnp.split(jnp.stack(phases), lax.axis_size('cols...  176 us
    add x6, other arithmetic, advance(): middle - jnp.abs(wind_x) * (middle - upwind_x)  107 us
    ppermute x16, starting transfers between devices, extended(): lax.ppermute(lax.slice_in_dim(block, block.shape[dim] - width, None, axis...  67.7 us
    all_to_all x1, waiting for transfers between devices, body(): lax.all_to_all(irradiance_layers, 'cols', split_axis=2, concat_axis=1, ti...  64.6 us
    another operation x2, other arithmetic, body(): jnp.stack(phases)  41.6 us
    unnamed x57, local copies, waits for them, and re-layouts  39.3 us
    ppermute x16, starting transfers between devices, extended(): lax.ppermute(lax.slice_in_dim(block, 0, width, axis=dim), axis, backward)  26.5 us
    all_to_all x1, local copies, waits for them, and re-layouts, body(): lax.all_to_all(irradiance_layers, 'cols', split_axis=2, concat_axis=1, ti...  18.6 us
  transfers between devices with their start and end apart: 34, of which 4 were waited for; matrix products, arithmetic and copies ran while one was open for 31% of the time, Pallas kernels for 0%

profile of v1, /device:TPU:3, one launch (start us, length us, event | category | flops | bytes accessed | tf_op | source)
XLA Modules:
  0.0 596.1 jit_solution(12879038088027218814)
XLA Ops:
  0.6 17.8 %copy.18 = bf16[2,64,16384]{1,0,2:T(2,128)(2,1)} copy(bf16[2,64,16384]{2,1,0:T(8,128)(2,1)} %param.7) | data formatting | bytes 8388608 | tf_op args[0]
  18.4 9.6 %reshape.52 = bf16[4,2,262144]{2,1,0:T(2,128)(2,1)} reshape(bf16[16384,2,64]{2,1,0:T(2,128)(2,1)} %bitcast.152) | data formatting | bytes 8388608
  27.9 5.0 all-to-all-start
  34.1 3.7 collective-permute-start.16
  37.8 1.9 collective-permute-start.17
  39.7 4.5 collective-permute-start
  44.3 1.9 collective-permute-start.1
  46.3 4.0 slice_bitcast_fusion.1
  50.5 3.6 collective-permute-start.18
  55.6 4.0 collective-permute-start.2
  60.9 64.6 %all-to-all-done = bf16[4,2,262144]{2,1,0:T(2,128)(2,1)} async-done(((bf16[4,2,262144]{2,1,0:T(2,128)(2,1)}), bf16[4,2,262144]{2,1,0:T(2,128)(2,1)}, u32[]{:S(2)}, u32[]{:S(2)}) %all-to-all-start) | async-done | bytes 4194336 | tf_op jit(solution)/shard_map/all_to_all | solution.py:52
  125.6 9.3 %reshape.53 = bf16[16384,2,64]{2,1,0:T(2,128)(2,1)} reshape(bf16[4,2,262144]{2,1,0:T(2,128)(2,1)} %all-to-all-done) | data formatting | bytes 8388608
  134.9 18.6 %copy.20 = bf16[2,64,4,4096]{3,1,2,0:T(8,128)(2,1)} copy(bf16[2,64,4,4096]{1,0,3,2:T(2,128)(2,1)} %bitcast.151) | data formatting | bytes 8388608 | tf_op jit(solution)/shard_map/all_to_all | solution.py:52
  153.5 4.2 fusion.22
  158.3 20.2 %add_add_fusion.3 = (f32[256,4096]{1,0:T(8,128)S(1)}, pred[256,4096]{1,0:T(8,128)(4,1)}, pred[256,4096]{1,0:T(8,128)(4,1)}) fusion(f32[256,4096]{1,0:T(8,128)} %copy-done.7, f32[1,4096]{1,0:T(1,128)S(1)} %collective-permute-done.16, f32[1,4096]{1,0:T(1,128)S(1)} %collective-permute-done.17, f32[258,1]{1,0:T(8,128)} %copy-done.10, f32[258,1]{1,0:T(8,128)} %copy-done.11, ...), kind=kLoop, calls=%fused_computation.82 | loop fusion | flops 36700160 | bytes 25205008 | tf_op jit(solution)/shard_map/add | solution.py:34
  178.5 5.7 collective-permute-start.20
  184.2 1.9 collective-permute-start.21
  186.2 19.6 %add_add_fusion.7 = (f32[256,4096]{1,0:T(8,128)S(1)}, pred[256,4096]{1,0:T(8,128)(4,1)}, pred[256,4096]{1,0:T(8,128)(4,1)}) fusion(f32[256,4096]{1,0:T(8,128)} %copy-done.6, f32[1,4096]{1,0:T(1,128)S(1)} %collective-permute-done, f32[1,4096]{1,0:T(1,128)S(1)} %collective-permute-done.1, f32[258,1]{1,0:T(8,128)S(1)} %collective-permute-done.2, ...), kind=kLoop, calls=%fused_computation.88 | loop fusion | flops 36700160 | bytes 25205008 | tf_op jit(solution)/shard_map/add | solution.py:34
  205.8 4.5 collective-permute-start.4
  210.4 1.9 collective-permute-start.5
  216.4 3.2 collective-permute-start.6
  222.3 12.5 %add_add_fusion.2 = f32[256,4096]{1,0:T(8,128)} fusion(f32[256,4096]{1,0:T(8,128)S(1)} %get-tuple-element.13, pred[256,4096]{1,0:T(8,128)(4,1)} %get-tuple-element.15, f32[1,4096]{1,0:T(1,128)S(1)} %collective-permute-done.20, f32[1,4096]{1,0:T(1,128)S(1)} %collective-permute-done.21, pred[256,4096]{1,0:T(8,128)(4,1)} %get-tuple-element.14, ...), kind=kLoop, calls=%fused_computation.81 | loop fusion | flops 34603008 | bytes 25205008 | tf_op jit(solution)/shard_map/add | solution.py:34
  234.8 1.6 fusion.24
  236.4 5.1 collective-permute-start.24
  241.5 1.9 collective-permute-start.25
  243.4 18.0 %add_add_fusion.6 = f32[256,4096]{1,0:T(8,128)} fusion(f32[256,4096]{1,0:T(8,128)} %copy-done, pred[256,4096]{1,0:T(8,128)(4,1)} %get-tuple-element.10, f32[1,4096]{1,0:T(1,128)S(1)} %collective-permute-done.4, f32[1,4096]{1,0:T(1,128)} %copy-done.15, pred[256,4096]{1,0:T(8,128)(4,1)} %get-tuple-element.9, f32[258,1]{1,0:T(8,128)S(1)} %collective-permute-done.6, ...), kind=kLoop, calls=%fused_computation.87 | loop fusion | flops 34603008 | bytes 25205008 | tf_op jit(solution)/shard_map/add | solution.py:34
  262.6 4.7 collective-permute-start.8
  267.3 1.9 collective-permute-start.9
  270.4 4.3 collective-permute-start.26
  276.1 4.0 collective-permute-start.10
  282.3 18.9 %add_add_fusion.1 = f32[256,4096]{1,0:T(8,128)} fusion(f32[256,4096]{1,0:T(8,128)} %add_add_fusion.2, pred[256,4096]{1,0:T(8,128)(4,1)} %get-tuple-element.15, f32[1,4096]{1,0:T(1,128)S(1)} %collective-permute-done.24, f32[1,4096]{1,0:T(1,128)S(1)} %collective-permute-done.25, pred[256,4096]{1,0:T(8,128)(4,1)} %get-tuple-element.14, f32[258,1]{1,0:T(8,128)} %copy-done.13, ...), kind=kLoop, calls=%fused_computation.80 | loop fusion | flops 34603008 | bytes 25205008 | tf_op jit(solution)/shard_map/add | solution.py:34
  301.2 1.6 fusion.23
  302.8 5.4 collective-permute-start.28
  308.2 1.9 collective-permute-start.29
  310.1 18.1 %add_add_fusion.5 = f32[256,4096]{1,0:T(8,128)} fusion(f32[256,4096]{1,0:T(8,128)} %add_add_fusion.6, pred[256,4096]{1,0:T(8,128)(4,1)} %get-tuple-element.10, f32[1,4096]{1,0:T(1,128)S(1)} %collective-permute-done.8, f32[1,4096]{1,0:T(1,128)} %copy-done.16, pred[256,4096]{1,0:T(8,128)(4,1)} %get-tuple-element.9, f32[258,1]{1,0:T(8,128)S(1)} %collective-permute-done.10, ...), kind=kLoop, calls=%fused_computation.86 | loop fusion | flops 34603008 | bytes 25205008 | tf_op jit(solution)/shard_map/add | solution.py:34
  329.4 4.7 collective-permute-start.12
  334.1 2.1 collective-permute-start.13
  337.3 4.3 collective-permute-start.30
  343.7 4.8 collective-permute-start.14
  348.5 1.8 collective-permute-start.15
  350.3 20.4 %multiply_bitcast_fusion = (f32[1,256,4096]{2,1,0:T(8,128)}, f32[256,4096]{1,0:T(8,128)}) fusion(f32[256,4096]{1,0:T(8,128)} %add_add_fusion.1, f32[256,4096]{1,0:T(8,128)S(1)} %get-tuple-element.13, f32[256,4096]{1,0:T(8,128)} %add_add_fusion.2, bf16[1,4,64,4096]{3,2,1,0:T(8,128)(2,1)} %copy-done.4, f32[2,256,4096]{2,1,0:T(8,128)} %param.11, ...), kind=kLoop, calls=%fused_computation.78 | loop fusion | flops 38797312 | bytes 37787920 | tf_op jit(solution)/shard_map/stack | solution.py:78
  370.8 21.2 %multiply_bitcast_fusion.1 = (f32[1,256,4096]{2,1,0:T(8,128)}, f32[256,4096]{1,0:T(8,128)}) fusion(f32[256,4096]{1,0:T(8,128)} %add_add_fusion.5, f32[256,4096]{1,0:T(8,128)S(1)} %copy-done.1, f32[256,4096]{1,0:T(8,128)} %add_add_fusion.6, bf16[1,4,64,4096]{3,2,1,0:T(8,128)(2,1)S(1)} %copy-done.3, f32[2,256,4096]{2,1,0:T(8,128)S(1)} %bitcast.148, ...), kind=kLoop, calls=%fused_computation.84 | loop fusion | flops 38797312 | bytes 37787920 | tf_op jit(solution)/shard_map/stack | solution.py:78
  391.9 2.6 fusion.11
  394.6 3.7 pad_maximum_fusion
  398.3 5.9 all-to-all-start.1
  404.2 7.9 %pad_maximum_fusion.1 = f32[2,256,4096]{2,1,0:T(8,128)} fusion(f32[1,256,4096]{2,1,0:T(8,128)} %bitcast.154, f32[1,256,4096]{2,1,0:T(8,128)} %bitcast.155), kind=kLoop, calls=%fused_computation.7 | loop fusion | flops 2097152 | bytes 16777216 | tf_op jit(solution)/shard_map/stack | solution.py:82
  412.0 176.1 %all-to-all-done.1 = f32[4,2,64,4096]{3,2,1,0:T(8,128)} async-done(((f32[4,2,64,4096]{3,2,1,0:T(8,128)}), f32[4,2,64,4096]{3,2,1,0:T(8,128)}, u32[]{:S(2)}, u32[]{:S(2)}) %all-to-all-start.1) | async-done | bytes 8388640 | tf_op jit(solution)/shard_map/all_to_all | solution.py:77
  588.1 7.8 %copy.24 = f32[4,2,8,8,4096]{4,3,0,2,1:T(8,128)} copy(f32[4,2,8,8,4096]{4,3,2,1,0:T(8,128)} %bitcast.27) | data formatting | bytes 16777216 | tf_op jit(solution)/shard_map/reshape | solution.py:76
  (113 shorter events, 21.7 us)
Async XLA Ops:
  27.9 97.6 %all-to-all-start = ((bf16[4,2,262144]{2,1,0:T(2,128)(2,1)}), bf16[4,2,262144]{2,1,0:T(2,128)(2,1)}, u32[]{:S(2)}, u32[]{:S(2)}) async-start(bf16[4,2,262144]{2,1,0:T(2,128)(2,1)} %reshape.52), calls=%async_computation | async-start | bytes 8388608 | tf_op jit(solution)/shard_map/all_to_all | solution.py:52
  34.1 16.3 %collective-permute-start.16 = (f32[1,4096]{1,0:T(1,128)S(1)}, f32[1,4096]{1,0:T(1,128)S(1)}, u32[]{:S(2)}, u32[]{:S(2)}) collective-permute-start(f32[1,4096]{1,0:T(1,128)S(1)} %get-tuple-element.23), channel_id=1, source_target_pairs={{0,4},{4,8},{8,12},{12,16},{16,20},{20,24},{24,28},{1,5},{5,9},{9,... | collective-permute-start | bytes 49160 | tf_op jit(solution)/shard_map/ppermute | solution.py:16
  37.8 12.6 %collective-permute-start.17 = (f32[1,4096]{1,0:T(1,128)S(1)}, f32[1,4096]{1,0:T(1,128)S(1)}, u32[]{:S(2)}, u32[]{:S(2)}) collective-permute-start(f32[1,4096]{1,0:T(1,128)S(1)} %get-tuple-element.22), channel_id=1, source_target_pairs={{4,0},{8,4},{12,8},{16,12},{20,16},{24,20},{28,24},{5,1},{9,5},{13... | collective-permute-start | bytes 49160 | tf_op jit(solution)/shard_map/ppermute | solution.py:19
  39.7 15.8 %collective-permute-start = (f32[1,4096]{1,0:T(1,128)S(1)}, f32[1,4096]{1,0:T(1,128)S(1)}, u32[]{:S(2)}, u32[]{:S(2)}) collective-permute-start(f32[1,4096]{1,0:T(1,128)S(1)} %get-tuple-element.21), channel_id=1, source_target_pairs={{0,4},{4,8},{8,12},{12,16},{16,20},{20,24},{24,28},{1,5},{5,9},{9,... | collective-permute-start | bytes 49160 | tf_op jit(solution)/shard_map/ppermute | solution.py:16
  44.3 11.2 %collective-permute-start.1 = (f32[1,4096]{1,0:T(1,128)S(1)}, f32[1,4096]{1,0:T(1,128)S(1)}, u32[]{:S(2)}, u32[]{:S(2)}) collective-permute-start(f32[1,4096]{1,0:T(1,128)S(1)} %get-tuple-element.20), channel_id=1, source_target_pairs={{4,0},{8,4},{12,8},{16,12},{20,16},{24,20},{28,24},{5,1},{9,5},{13... | collective-permute-start | bytes 49160 | tf_op jit(solution)/shard_map/ppermute | solution.py:19
  50.5 107.1 %collective-permute-start.18 = (f32[258,1]{1,0:T(8,128)S(1)}, f32[258,1]{1,0:T(8,128)S(1)}, u32[]{:S(2)}, u32[]{:S(2)}) collective-permute-start(f32[258,1]{1,0:T(8,128)S(1)} %get-tuple-element.41), channel_id=1, source_target_pairs={{0,1},{1,2},{2,3},{4,5},{5,6},{6,7},{8,9},{9,10},{10,11},{12,13},{... | collective-permute-start | bytes 3104 | tf_op jit(solution)/shard_map/ppermute | solution.py:16
  54.2 103.4 %collective-permute-start.19 = (f32[258,1]{1,0:T(8,128)S(1)}, f32[258,1]{1,0:T(8,128)S(1)}, u32[]{:S(2)}, u32[]{:S(2)}) collective-permute-start(f32[258,1]{1,0:T(8,128)S(1)} %get-tuple-element.40), channel_id=1, source_target_pairs={{1,0},{2,1},{3,2},{5,4},{6,5},{7,6},{9,8},{10,9},{11,10},{13,12},{... | collective-permute-start | bytes 3104 | tf_op jit(solution)/shard_map/ppermute | solution.py:19
  55.6 130.5 %collective-permute-start.2 = (f32[258,1]{1,0:T(8,128)S(1)}, f32[258,1]{1,0:T(8,128)S(1)}, u32[]{:S(2)}, u32[]{:S(2)}) collective-permute-start(f32[258,1]{1,0:T(8,128)S(1)} %get-tuple-element.33), channel_id=1, source_target_pairs={{0,1},{1,2},{2,3},{4,5},{5,6},{6,7},{8,9},{9,10},{10,11},{12,13},{... | collective-permute-start | bytes 3104 | tf_op jit(solution)/shard_map/ppermute | solution.py:16
  59.6 126.5 %collective-permute-start.3 = (f32[258,1]{1,0:T(8,128)S(1)}, f32[258,1]{1,0:T(8,128)}, u32[]{:S(2)}, u32[]{:S(2)}) collective-permute-start(f32[258,1]{1,0:T(8,128)S(1)} %get-tuple-element.32), channel_id=1, source_target_pairs={{1,0},{2,1},{3,2},{5,4},{6,5},{7,6},{9,8},{10,9},{11,10},{13,12},{... | collective-permute-start | bytes 3104 | tf_op jit(solution)/shard_map/ppermute | solution.py:19
  153.4 32.7 %slice-start = ((s8[8388608]{0:T(1024)(128)(4,1)}), s8[4194304]{0:T(1024)(128)(4,1)S(1)}, s32[]{:S(2)}) async-start(s8[8388608]{0:T(1024)(128)(4,1)} %bitcast.143), calls=%async_computation.2 | async-start | bytes 8388608
  153.4 32.7 %slice-start.2 = ((s8[8388608]{0:T(1024)(128)(4,1)}), s8[4194304]{0:T(1024)(128)(4,1)S(1)}, s32[]{:S(2)}) async-start(s8[8388608]{0:T(1024)(128)(4,1)} %bitcast.145), calls=%async_computation.4 | async-start | bytes 8388608
  153.5 32.7 %slice-start.6 = ((s8[8388608]{0:T(1024)(128)(4,1)}), s8[4194304]{0:T(1024)(128)(4,1)S(1)}, s32[]{:S(2)}) async-start(s8[8388608]{0:T(1024)(128)(4,1)} %bitcast.149), calls=%async_computation.8 | async-start | bytes 8388608
  157.6 20.9 %copy-start.4 = (bf16[1,4,64,4096]{3,2,1,0:T(8,128)(2,1)}, bf16[1,4,64,4096]{3,2,1,0:T(8,128)(2,1)S(1)}, u32[]{:S(2)}) copy-start(bf16[1,4,64,4096]{3,2,1,0:T(8,128)(2,1)S(1)} %get-tuple-element.49) | copy-start | bytes 6291460
  158.3 27.9 %slice-start.1 = ((s8[8388608]{0:T(1024)(128)(4,1)}), s8[4194304]{0:T(1024)(128)(4,1)S(1)}, s32[]{:S(2)}) async-start(s8[8388608]{0:T(1024)(128)(4,1)} %bitcast.143), calls=%async_computation.3 | async-start | bytes 8388608
  158.3 27.9 %slice-start.3 = ((s8[8388608]{0:T(1024)(128)(4,1)}), s8[4194304]{0:T(1024)(128)(4,1)S(1)}, s32[]{:S(2)}) async-start(s8[8388608]{0:T(1024)(128)(4,1)} %bitcast.145), calls=%async_computation.5 | async-start | bytes 8388608
  158.3 27.9 %slice-start.7 = ((s8[8388608]{0:T(1024)(128)(4,1)}), s8[4194304]{0:T(1024)(128)(4,1)S(1)}, s32[]{:S(2)}) async-start(s8[8388608]{0:T(1024)(128)(4,1)} %bitcast.149), calls=%async_computation.9 | async-start | bytes 8388608
  178.5 33.8 %collective-permute-start.20 = (f32[1,4096]{1,0:T(1,128)S(1)}, f32[1,4096]{1,0:T(1,128)S(1)}, u32[]{:S(2)}, u32[]{:S(2)}) collective-permute-start(f32[1,4096]{1,0:T(1,128)S(1)} %get-tuple-element.55), channel_id=1, source_target_pairs={{0,4},{4,8},{8,12},{12,16},{16,20},{20,24},{24,28},{1,5},{5,9},{9,... | collective-permute-start | bytes 49160 | tf_op jit(solution)/shard_map/ppermute | solution.py:16
  184.2 28.1 %collective-permute-start.21 = (f32[1,4096]{1,0:T(1,128)S(1)}, f32[1,4096]{1,0:T(1,128)S(1)}, u32[]{:S(2)}, u32[]{:S(2)}) collective-permute-start(f32[1,4096]{1,0:T(1,128)S(1)} %get-tuple-element.54), channel_id=1, source_target_pairs={{4,0},{8,4},{12,8},{16,12},{20,16},{24,20},{28,24},{5,1},{9,5},{13... | collective-permute-start | bytes 49160 | tf_op jit(solution)/shard_map/ppermute | solution.py:19
  205.8 9.2 %collective-permute-start.4 = (f32[1,4096]{1,0:T(1,128)S(1)}, f32[1,4096]{1,0:T(1,128)S(1)}, u32[]{:S(2)}, u32[]{:S(2)}) collective-permute-start(f32[1,4096]{1,0:T(1,128)S(1)} %get-tuple-element.47), channel_id=1, source_target_pairs={{0,4},{4,8},{8,12},{12,16},{16,20},{20,24},{24,28},{1,5},{5,9},{9,... | collective-permute-start | bytes 49160 | tf_op jit(solution)/shard_map/ppermute | solution.py:16
  210.4 6.0 collective-permute-start.5
  212.4 8.5 %collective-permute-start.22 = (f32[258,1]{1,0:T(8,128)S(1)}, f32[258,1]{1,0:T(8,128)S(1)}, u32[]{:S(2)}, u32[]{:S(2)}) collective-permute-start(f32[258,1]{1,0:T(8,128)S(1)} %get-tuple-element.39), channel_id=1, source_target_pairs={{0,1},{1,2},{2,3},{4,5},{5,6},{6,7},{8,9},{9,10},{10,11},{12,13},{... | collective-permute-start | bytes 3104 | tf_op jit(solution)/shard_map/ppermute | solution.py:16
  213.7 7.3 %collective-permute-start.23 = (f32[258,1]{1,0:T(8,128)S(1)}, f32[258,1]{1,0:T(8,128)S(1)}, u32[]{:S(2)}, u32[]{:S(2)}) collective-permute-start(f32[258,1]{1,0:T(8,128)S(1)} %get-tuple-element.38), channel_id=1, source_target_pairs={{1,0},{2,1},{3,2},{5,4},{6,5},{7,6},{9,8},{10,9},{11,10},{13,12},{... | collective-permute-start | bytes 3104 | tf_op jit(solution)/shard_map/ppermute | solution.py:19
  216.3 18.4 %copy-start.15 = (f32[1,4096]{1,0:T(1,128)}, f32[1,4096]{1,0:T(1,128)S(1)}, u32[]{:S(2)}) copy-start(f32[1,4096]{1,0:T(1,128)S(1)} %collective-permute-done.5) | copy-start | bytes 49156
  216.4 27.0 %collective-permute-start.6 = (f32[258,1]{1,0:T(8,128)S(1)}, f32[258,1]{1,0:T(8,128)S(1)}, u32[]{:S(2)}, u32[]{:S(2)}) collective-permute-start(f32[258,1]{1,0:T(8,128)S(1)} %get-tuple-element.31), channel_id=1, source_target_pairs={{0,1},{1,2},{2,3},{4,5},{5,6},{6,7},{8,9},{9,10},{10,11},{12,13},{... | collective-permute-start | bytes 3104 | tf_op jit(solution)/shard_map/ppermute | solution.py:16
  219.7 23.8 %collective-permute-start.7 = (f32[258,1]{1,0:T(8,128)S(1)}, f32[258,1]{1,0:T(8,128)}, u32[]{:S(2)}, u32[]{:S(2)}) collective-permute-start(f32[258,1]{1,0:T(8,128)S(1)} %get-tuple-element.30), channel_id=1, source_target_pairs={{1,0},{2,1},{3,2},{5,4},{6,5},{7,6},{9,8},{10,9},{11,10},{13,12},{... | collective-permute-start | bytes 3104 | tf_op jit(solution)/shard_map/ppermute | solution.py:19
  236.4 32.9 %collective-permute-start.24 = (f32[1,4096]{1,0:T(1,128)}, f32[1,4096]{1,0:T(1,128)S(1)}, u32[]{:S(2)}, u32[]{:S(2)}) collective-permute-start(f32[1,4096]{1,0:T(1,128)} %get-tuple-element.53), channel_id=1, source_target_pairs={{0,4},{4,8},{8,12},{12,16},{16,20},{20,24},{24,28},{1,5},{5,9},{9,... | collective-permute-start | bytes 49160 | tf_op jit(solution)/shard_map/ppermute | solution.py:16
  241.5 27.8 %collective-permute-start.25 = (f32[1,4096]{1,0:T(1,128)}, f32[1,4096]{1,0:T(1,128)S(1)}, u32[]{:S(2)}, u32[]{:S(2)}) collective-permute-start(f32[1,4096]{1,0:T(1,128)} %get-tuple-element.52), channel_id=1, source_target_pairs={{4,0},{8,4},{12,8},{16,12},{20,16},{24,20},{28,24},{5,1},{9,5},{13... | collective-permute-start | bytes 49160 | tf_op jit(solution)/shard_map/ppermute | solution.py:19
  262.6 13.3 %collective-permute-start.8 = (f32[1,4096]{1,0:T(1,128)S(1)}, f32[1,4096]{1,0:T(1,128)S(1)}, u32[]{:S(2)}, u32[]{:S(2)}) collective-permute-start(f32[1,4096]{1,0:T(1,128)S(1)} %get-tuple-element.45), channel_id=1, source_target_pairs={{0,4},{4,8},{8,12},{12,16},{16,20},{20,24},{24,28},{1,5},{5,9},{9,... | collective-permute-start | bytes 49160 | tf_op jit(solution)/shard_map/ppermute | solution.py:16
  267.3 8.6 %collective-permute-start.9 = (f32[1,4096]{1,0:T(1,128)S(1)}, f32[1,4096]{1,0:T(1,128)S(1)}, u32[]{:S(2)}, u32[]{:S(2)}) collective-permute-start(f32[1,4096]{1,0:T(1,128)S(1)} %get-tuple-element.44), channel_id=1, source_target_pairs={{4,0},{8,4},{12,8},{16,12},{20,16},{24,20},{28,24},{5,1},{9,5},{13... | collective-permute-start | bytes 49160 | tf_op jit(solution)/shard_map/ppermute | solution.py:19
  270.4 11.2 %collective-permute-start.26 = (f32[258,1]{1,0:T(8,128)S(1)}, f32[258,1]{1,0:T(8,128)S(1)}, u32[]{:S(2)}, u32[]{:S(2)}) collective-permute-start(f32[258,1]{1,0:T(8,128)S(1)} %get-tuple-element.37), channel_id=1, source_target_pairs={{0,1},{1,2},{2,3},{4,5},{5,6},{6,7},{8,9},{9,10},{10,11},{12,13},{... | collective-permute-start | bytes 3104 | tf_op jit(solution)/shard_map/ppermute | solution.py:16
  274.6 7.6 %collective-permute-start.27 = (f32[258,1]{1,0:T(8,128)S(1)}, f32[258,1]{1,0:T(8,128)}, u32[]{:S(2)}, u32[]{:S(2)}) collective-permute-start(f32[258,1]{1,0:T(8,128)S(1)} %get-tuple-element.36), channel_id=1, source_target_pairs={{1,0},{2,1},{3,2},{5,4},{6,5},{7,6},{9,8},{10,9},{11,10},{13,12},{... | collective-permute-start | bytes 3104 | tf_op jit(solution)/shard_map/ppermute | solution.py:19
  276.0 25.2 %copy-start.16 = (f32[1,4096]{1,0:T(1,128)}, f32[1,4096]{1,0:T(1,128)S(1)}, u32[]{:S(2)}) copy-start(f32[1,4096]{1,0:T(1,128)S(1)} %collective-permute-done.9) | copy-start | bytes 49156
  276.1 34.0 %collective-permute-start.10 = (f32[258,1]{1,0:T(8,128)S(1)}, f32[258,1]{1,0:T(8,128)S(1)}, u32[]{:S(2)}, u32[]{:S(2)}) collective-permute-start(f32[258,1]{1,0:T(8,128)S(1)} %get-tuple-element.29), channel_id=1, source_target_pairs={{0,1},{1,2},{2,3},{4,5},{5,6},{6,7},{8,9},{9,10},{10,11},{12,13},{... | collective-permute-start | bytes 3104 | tf_op jit(solution)/shard_map/ppermute | solution.py:16
  280.1 30.0 %collective-permute-start.11 = (f32[258,1]{1,0:T(8,128)S(1)}, f32[258,1]{1,0:T(8,128)}, u32[]{:S(2)}, u32[]{:S(2)}) collective-permute-start(f32[258,1]{1,0:T(8,128)S(1)} %get-tuple-element.28), channel_id=1, source_target_pairs={{1,0},{2,1},{3,2},{5,4},{6,5},{7,6},{9,8},{10,9},{11,10},{13,12},{... | collective-permute-start | bytes 3104 | tf_op jit(solution)/shard_map/ppermute | solution.py:19
  302.8 33.4 %collective-permute-start.28 = (f32[1,4096]{1,0:T(1,128)}, f32[1,4096]{1,0:T(1,128)S(1)}, u32[]{:S(2)}, u32[]{:S(2)}) collective-permute-start(f32[1,4096]{1,0:T(1,128)} %get-tuple-element.50), channel_id=1, source_target_pairs={{0,4},{4,8},{8,12},{12,16},{16,20},{20,24},{24,28},{1,5},{5,9},{9,... | collective-permute-start | bytes 49160 | tf_op jit(solution)/shard_map/ppermute | solution.py:16
  308.2 28.0 %collective-permute-start.29 = (f32[1,4096]{1,0:T(1,128)}, f32[1,4096]{1,0:T(1,128)S(1)}, u32[]{:S(2)}, u32[]{:S(2)}) collective-permute-start(f32[1,4096]{1,0:T(1,128)} %get-tuple-element.51), channel_id=1, source_target_pairs={{4,0},{8,4},{12,8},{16,12},{20,16},{24,20},{28,24},{5,1},{9,5},{13... | collective-permute-start | bytes 49160 | tf_op jit(solution)/shard_map/ppermute | solution.py:19
  329.4 13.4 %collective-permute-start.12 = (f32[1,4096]{1,0:T(1,128)S(1)}, f32[1,4096]{1,0:T(1,128)S(1)}, u32[]{:S(2)}, u32[]{:S(2)}) collective-permute-start(f32[1,4096]{1,0:T(1,128)S(1)} %get-tuple-element.42), channel_id=1, source_target_pairs={{0,4},{4,8},{8,12},{12,16},{16,20},{20,24},{24,28},{1,5},{5,9},{9,... | collective-permute-start | bytes 49160 | tf_op jit(solution)/shard_map/ppermute | solution.py:16
  334.1 8.8 %collective-permute-start.13 = (f32[1,4096]{1,0:T(1,128)S(1)}, f32[1,4096]{1,0:T(1,128)S(1)}, u32[]{:S(2)}, u32[]{:S(2)}) collective-permute-start(f32[1,4096]{1,0:T(1,128)S(1)} %get-tuple-element.43), channel_id=1, source_target_pairs={{4,0},{8,4},{12,8},{16,12},{20,16},{24,20},{28,24},{5,1},{9,5},{13... | collective-permute-start | bytes 49160 | tf_op jit(solution)/shard_map/ppermute | solution.py:19
  337.3 13.0 %collective-permute-start.30 = (f32[258,1]{1,0:T(8,128)S(1)}, f32[258,1]{1,0:T(8,128)S(1)}, u32[]{:S(2)}, u32[]{:S(2)}) collective-permute-start(f32[258,1]{1,0:T(8,128)S(1)} %get-tuple-element.34), channel_id=1, source_target_pairs={{0,1},{1,2},{2,3},{4,5},{5,6},{6,7},{8,9},{9,10},{10,11},{12,13},{... | collective-permute-start | bytes 3104 | tf_op jit(solution)/shard_map/ppermute | solution.py:16
  341.6 8.7 %collective-permute-start.31 = (f32[258,1]{1,0:T(8,128)S(1)}, f32[258,1]{1,0:T(8,128)S(1)}, u32[]{:S(2)}, u32[]{:S(2)}) collective-permute-start(f32[258,1]{1,0:T(8,128)S(1)} %get-tuple-element.35), channel_id=1, source_target_pairs={{1,0},{2,1},{3,2},{5,4},{6,5},{7,6},{9,8},{10,9},{11,10},{13,12},{... | collective-permute-start | bytes 3104 | tf_op jit(solution)/shard_map/ppermute | solution.py:19
  343.7 27.0 %collective-permute-start.14 = (f32[258,1]{1,0:T(8,128)}, f32[258,1]{1,0:T(8,128)S(1)}, u32[]{:S(2)}, u32[]{:S(2)}) collective-permute-start(f32[258,1]{1,0:T(8,128)} %get-tuple-element.26), channel_id=1, source_target_pairs={{0,1},{1,2},{2,3},{4,5},{5,6},{6,7},{8,9},{9,10},{10,11},{12,13},{... | collective-permute-start | bytes 3104 | tf_op jit(solution)/shard_map/ppermute | solution.py:16
  348.4 22.3 %slice-start.4 = ((s8[8388608]{0:T(1024)(128)(4,1)}), s8[4194304]{0:T(1024)(128)(4,1)S(1)}, s32[]{:S(2)}) async-start(s8[8388608]{0:T(1024)(128)(4,1)} %bitcast.147), calls=%async_computation.6 | async-start | bytes 8388608
  348.4 22.3 %slice-start.5 = ((s8[8388608]{0:T(1024)(128)(4,1)}), s8[4194304]{0:T(1024)(128)(4,1)S(1)}, s32[]{:S(2)}) async-start(s8[8388608]{0:T(1024)(128)(4,1)} %bitcast.147), calls=%async_computation.7 | async-start | bytes 8388608
  348.5 22.3 %copy-start.1 = (f32[256,4096]{1,0:T(8,128)S(1)}, f32[256,4096]{1,0:T(8,128)}, u32[]{:S(2)}) copy-start(f32[256,4096]{1,0:T(8,128)} %copy-done) | copy-start | bytes 12582916
  348.5 22.3 %copy-start.3 = (bf16[1,4,64,4096]{3,2,1,0:T(8,128)(2,1)S(1)}, bf16[1,4,64,4096]{3,2,1,0:T(8,128)(2,1)}, u32[]{:S(2)}) copy-start(bf16[1,4,64,4096]{3,2,1,0:T(8,128)(2,1)} %get-tuple-element.48) | copy-start | bytes 6291460
  348.5 22.2 %collective-permute-start.15 = (f32[258,1]{1,0:T(8,128)}, f32[258,1]{1,0:T(8,128)S(1)}, u32[]{:S(2)}, u32[]{:S(2)}) collective-permute-start(f32[258,1]{1,0:T(8,128)} %get-tuple-element.27), channel_id=1, source_target_pairs={{1,0},{2,1},{3,2},{5,4},{6,5},{7,6},{9,8},{10,9},{11,10},{13,12},{... | collective-permute-start | bytes 3104 | tf_op jit(solution)/shard_map/ppermute | solution.py:19
  370.7 21.2 %copy-start.9 = (f32[1,256,4096]{2,1,0:T(8,128)S(1)}, f32[1,256,4096]{2,1,0:T(8,128)}, u32[]{:S(2)}) copy-start(f32[1,256,4096]{2,1,0:T(8,128)} %get-tuple-element.11) | copy-start | bytes 12582916
  398.3 189.9 %all-to-all-start.1 = ((f32[4,2,64,4096]{3,2,1,0:T(8,128)}), f32[4,2,64,4096]{3,2,1,0:T(8,128)}, u32[]{:S(2)}, u32[]{:S(2)}) async-start(f32[4,2,64,4096]{3,2,1,0:T(8,128)} %pad_maximum_fusion), calls=%async_computation.1 | async-start | bytes 16777216 | tf_op jit(solution)/shard_map/all_to_all | solution.py:77
  (13 other events, 91.9 us)
